TPU v7x, 128 devices: a whole 4x4x4 slice. The times are simulated.
128 devices in a mesh: section: 16 (over z_hi, y, core), seq: 8 (over x, z_lo).
Axes of the slice: x: 4, y: 4, z: 4 (z_hi: 2, z_lo: 2; z = z_hi * 2 + z_lo), core: 2. Of those that a mesh axis runs over, the one named last changes fastest.
Arguments:
- forward_rows: bfloat16 [16, 1024, 4096], P('section', 'seq'), may hold values from -54 to 54
- saved_rows: bfloat16 [16, 1024, 4096], P('section', 'seq'), may hold values from -54 to 54
- output_grad: bfloat16 [16, 1024, 4096], P('section', 'seq'), may hold values from -6 to 6
- forward_docs: int32 [16, 1024], replicated, may hold values from 0 to 3, never falling along the last dimension, each value on 1 to 512 neighbouring positions
- backward_docs: int32 [16, 1024], replicated, may hold values from 0 to 3, never falling along the last dimension, each value on 1 to 512 neighbouring positions
- norm_gain: float32 [16, 4096], P('section'), may hold values from 0.7 to 8
- query_weight: bfloat16 [16, 4096, 4096], P('section', None, 'seq'), may hold values from -0.09375 to 0.09375
- key_matrix: bfloat16 [16, 4096, 1024], P('section', None, 'seq'), may hold values from -0.09375 to 0.09375
- value_matrix: bfloat16 [16, 4096, 1024], P('section', None, 'seq'), may hold values from -0.09375 to 0.09375
Outputs:
- section_output: bfloat16 [16, 1024, 4096], P('section', 'seq')
- input_grad: bfloat16 [16, 1024, 4096], P('section', 'seq')
Inputs may be any that keep to these rules, and one draw needn't show every extreme that they name: `forward_docs`: document ids never fall along a row; every document holds at most 512 tokens and some document of each row holds exactly that many. `backward_docs`: document ids never fall along a row; every document holds at most 512 tokens and some document of each row holds exactly that many.
All inputs are finite; a program needn't handle non-finite values.
Results may differ from a plain program's by a relative error of at most 0.017.
The roundings to bfloat16 on the way count: a program that leaves them out, or rounds other values in their place, can miss the bound.
Values may be sent and summed in bfloat16 or wider, within the bound.
A program may use at most 192 MiB of HBM per device.

v0:
```python
import jax
import jax.numpy as jnp
from jax import lax
from jax.sharding import PartitionSpec as P

MODEL_WIDTH = 4096
HEAD_SIZE = 128
epsilon = 1e-05
rope_base = 500000.0


def passed_along(shard, axis, by):
    peers = lax.axis_size(axis)
    pairs = [(i, i + by) for i in range(peers) if 0 <= i + by < peers]
    return lax.ppermute(shard, axis, pairs)


def rotation_tables(positions):
    half = HEAD_SIZE // 2
    freqs = rope_base ** (-(jnp.arange(half, dtype=jnp.float32) * 2.0 / HEAD_SIZE))
    angles = positions[:, None] * freqs[None, :]
    return (jnp.cos(angles), jnp.sin(angles))


def rotate(values, cosines, sines, sign):
    half = values.shape[-1] // 2
    extra = (1,) * (values.ndim - 2)
    cos_wide = cosines.reshape(cosines.shape[:1] + extra + cosines.shape[1:])
    sin_wide = sines.reshape(sines.shape[:1] + extra + sines.shape[1:])
    first = values[..., :half]
    second = values[..., half:]
    return jnp.concatenate(
        [first * cos_wide - sign * second * sin_wide, second * cos_wide + sign * first * sin_wide],
        axis=-1,
    )


def pair_mask(row_docs, col_docs, row_begin):
    row_pos = row_begin + lax.iota(jnp.int32, row_docs.shape[0])
    col_pos = lax.iota(jnp.int32, col_docs.shape[0])
    return (col_pos[None, :] <= row_pos[:, None]) & (row_docs[:, None] == col_docs[None, :])


def block_probs(query_block, key_heads, allowed):
    scores = jnp.einsum(
        "tjgd,sjd->jgts", query_block, key_heads, preferred_element_type=jnp.float32
    ) * HEAD_SIZE ** (-0.5)
    scores = jnp.where(allowed, scores, -1e30)
    row_top = jnp.max(scores, axis=-1, keepdims=True)
    exp_scores = jnp.where(allowed, jnp.exp(scores - row_top), 0.0)
    return exp_scores / jnp.sum(exp_scores, axis=-1, keepdims=True)


def attend(query_rows_local, key_rows, value_rows, documents):
    sequence_length = query_rows_local.shape[0]
    groups = key_rows.shape[1] // HEAD_SIZE
    group_size = query_rows_local.shape[1] // key_rows.shape[1]
    query_head_count = query_rows_local.reshape(sequence_length, groups, group_size, HEAD_SIZE)
    key_heads = key_rows.reshape(sequence_length, groups, HEAD_SIZE)
    value_heads = value_rows.reshape(sequence_length, groups, HEAD_SIZE)
    block_rows = min(512, sequence_length)
    pieces = []
    for block_index in range(sequence_length // block_rows):
        begin_row = block_index * block_rows
        end_row = begin_row + block_rows
        allowed = pair_mask(documents[begin_row:end_row], documents[:end_row], begin_row)
        probability = block_probs(
            query_head_count[begin_row:end_row], key_heads[:end_row], allowed
        ).astype(jnp.bfloat16)
        mixed_rows = jnp.einsum(
            "jgts,sjd->tjgd", probability, value_heads[:end_row], preferred_element_type=jnp.float32
        )
        pieces.append(mixed_rows.astype(jnp.bfloat16))
    return lax.optimization_barrier(
        jnp.concatenate(pieces, 0).reshape(sequence_length, query_rows_local.shape[1])
    )


def attend_back(query_rows_local, key_rows, value_rows, output_gradient, documents, cosines, sines):
    sequence_length = query_rows_local.shape[0]
    groups = key_rows.shape[1] // HEAD_SIZE
    group_size = query_rows_local.shape[1] // key_rows.shape[1]
    query_head_count = query_rows_local.reshape(sequence_length, groups, group_size, HEAD_SIZE)
    key_heads = key_rows.reshape(sequence_length, groups, HEAD_SIZE)
    value_heads = value_rows.reshape(sequence_length, groups, HEAD_SIZE)
    head_gradients = output_gradient.reshape(sequence_length, groups, group_size, HEAD_SIZE)
    scale = HEAD_SIZE ** (-0.5)
    key_grad = jnp.zeros((sequence_length, groups, HEAD_SIZE), jnp.float32)
    value_grad = jnp.zeros((sequence_length, groups, HEAD_SIZE), jnp.float32)
    block_rows = min(512, sequence_length)
    query_pieces = []
    for block_index in range(sequence_length // block_rows):
        begin_row = block_index * block_rows
        end_row = begin_row + block_rows
        allowed = pair_mask(documents[begin_row:end_row], documents[:end_row], begin_row)
        query_block = query_head_count[begin_row:end_row]
        grad_block = head_gradients[begin_row:end_row]
        probability = block_probs(query_block, key_heads[:end_row], allowed)
        grad_probs = jnp.einsum(
            "tjgd,sjd->jgts", grad_block, value_heads[:end_row], preferred_element_type=jnp.float32
        )
        row_delta = jnp.sum(probability * grad_probs, axis=-1, keepdims=True)
        grad_scores = (probability * (grad_probs - row_delta)).astype(jnp.bfloat16)
        query_piece = (
            jnp.einsum(
                "jgts,sjd->tjgd",
                grad_scores,
                key_heads[:end_row],
                preferred_element_type=jnp.float32,
            )
            * scale
        )
        query_piece = rotate(
            query_piece, cosines[begin_row:end_row], sines[begin_row:end_row], -1.0
        )
        query_pieces.append(query_piece.astype(jnp.bfloat16))
        key_grad = key_grad.at[:end_row].add(
            jnp.einsum(
                "jgts,tjgd->sjd", grad_scores, query_block, preferred_element_type=jnp.float32
            )
            * scale
        )
        value_grad = value_grad.at[:end_row].add(
            jnp.einsum(
                "jgts,tjgd->sjd",
                probability.astype(jnp.bfloat16),
                grad_block,
                preferred_element_type=jnp.float32,
            )
        )
    query_grad = jnp.concatenate(query_pieces, 0).reshape(
        sequence_length, query_rows_local.shape[1]
    )
    key_grad = (
        rotate(key_grad, cosines, sines, -1.0)
        .astype(jnp.bfloat16)
        .reshape(sequence_length, groups * HEAD_SIZE)
    )
    value_grad = value_grad.astype(jnp.bfloat16).reshape(sequence_length, groups * HEAD_SIZE)
    return lax.optimization_barrier((query_grad, key_grad, value_grad))


def token_scale(hidden):
    return lax.rsqrt(jnp.mean(hidden * hidden, axis=-1, keepdims=True) + epsilon)


def heads_inputs(rows_whole, weights):
    query_weight, key_matrix, value_matrix = weights
    sequence_length = rows_whole.shape[0]
    cosines, sines = rotation_tables(jnp.arange(sequence_length, dtype=jnp.float32))
    query_proj = jnp.dot(rows_whole, query_weight, preferred_element_type=jnp.float32)
    key_projected_rows = jnp.dot(rows_whole, key_matrix, preferred_element_type=jnp.float32)
    value_projected_rows = jnp.dot(rows_whole, value_matrix, preferred_element_type=jnp.float32)
    query_rows_local = (
        rotate(query_proj.reshape(sequence_length, -1, HEAD_SIZE), cosines, sines, 1.0)
        .reshape(sequence_length, -1)
        .astype(jnp.bfloat16)
    )
    key_rows = (
        rotate(key_projected_rows.reshape(sequence_length, -1, HEAD_SIZE), cosines, sines, 1.0)
        .reshape(sequence_length, -1)
        .astype(jnp.bfloat16)
    )
    value_rows = value_projected_rows.astype(jnp.bfloat16)
    return (query_rows_local, key_rows, value_rows, cosines, sines)


def body(
    forward_rows,
    saved_rows,
    output_grad,
    forward_docs,
    backward_docs,
    norm_gain,
    query_weight,
    key_matrix,
    value_matrix,
):
    section_index = lax.axis_index("section")
    first_docs = lax.dynamic_index_in_dim(forward_docs, section_index, 0, keepdims=False)
    back_docs = lax.dynamic_index_in_dim(backward_docs, section_index, 0, keepdims=False)
    gain_row = norm_gain[0]
    weights = (query_weight[0], key_matrix[0], value_matrix[0])
    forward_hidden = forward_rows[0].astype(jnp.float32)
    forward_normed = (forward_hidden * token_scale(forward_hidden) * gain_row).astype(jnp.bfloat16)
    back_hidden = saved_rows[0].astype(jnp.float32)
    back_scale = token_scale(back_hidden)
    back_normed = (back_hidden * back_scale * gain_row).astype(jnp.bfloat16)
    forward_whole = lax.all_gather(forward_normed, "seq", axis=0, tiled=True)
    query_rows_local, key_rows, value_rows, cosines, sines = heads_inputs(forward_whole, weights)
    mixed_rows = attend(query_rows_local, key_rows, value_rows, first_docs)
    mixed_rows = lax.all_to_all(mixed_rows, "seq", split_axis=0, concat_axis=1, tiled=True)
    first_out = (forward_hidden + mixed_rows.astype(jnp.float32)).astype(jnp.bfloat16)
    section_output = passed_along(first_out, "section", 1)
    back_whole = lax.all_gather(back_normed, "seq", axis=0, tiled=True)
    head_gradients = lax.all_to_all(output_grad[0], "seq", split_axis=1, concat_axis=0, tiled=True)
    query_rows_local, key_rows, value_rows, cosines, sines = heads_inputs(back_whole, weights)
    query_grad, key_grad, value_grad = attend_back(
        query_rows_local, key_rows, value_rows, head_gradients, back_docs, cosines, sines
    )
    term = jnp.einsum("tc,rc->tr", query_grad, weights[0], preferred_element_type=jnp.float32)
    term = term + jnp.einsum("tc,rc->tr", key_grad, weights[1], preferred_element_type=jnp.float32)
    input_sum = lax.psum_scatter(
        (
            term
            + jnp.einsum("tc,rc->tr", value_grad, weights[2], preferred_element_type=jnp.float32)
        ).astype(jnp.bfloat16),
        "seq",
        scatter_dimension=0,
        tiled=True,
    ).astype(jnp.float32)
    gained = gain_row * input_sum
    inner_sum = jnp.sum(back_hidden * gained, axis=-1, keepdims=True)
    norm_part = (
        back_scale * gained
        - back_hidden * (back_scale * back_scale * back_scale) * inner_sum / MODEL_WIDTH
    )
    first_grad = (output_grad[0].astype(jnp.float32) + norm_part).astype(jnp.bfloat16)
    input_grad = passed_along(first_grad, "section", -1)
    return (section_output[None], input_grad[None])


def solution(mesh):
    placed = (
        P("section", "seq", None),
        P("section", "seq", None),
        P("section", "seq", None),
        P(),
        P(),
        P("section", None),
        P("section", None, "seq"),
        P("section", None, "seq"),
        P("section", None, "seq"),
    )
    return jax.shard_map(
        body,
        mesh=mesh,
        in_specs=placed,
        out_specs=(P("section", "seq", None), P("section", "seq", None)),
        check_vma=False,
    )
```

profile of v0, /device:TPU:1, one launch (start us, length us, event | category | flops | bytes accessed | tf_op | source)
XLA Modules:
  0.0 678.1 jit_solution(13444456036712751143)
XLA Ops:
  7.2 1.7 fusion.29
  8.9 1.5 fusion.33
  10.9 0.6 copy-done.20
  11.5 3.5 fusion.35
  15.1 0.7 all-gather.3.cloned.1.call-update
  16.2 1.4 copy.43
  17.6 6.2 all-to-all-start.1
  23.8 0.6 reduce-scatter.2.cloned.1.call-start
  24.3 6.4 copy.76
  30.7 0.8 constant_dynamic-slice_fusion.2
  31.5 0.9 constant_dynamic-slice_fusion
  32.6 1.0 fusion.112
  33.6 0.8 slice_multiply_fusion.1
  34.4 1.7 fusion.48
  36.1 6.0 all-to-all-done.1
  42.1 1.1 fusion.146
  43.2 2.0 reshape.530
  45.2 2.0 reshape.532
  47.1 148.6 %all-gather.5.cloned.1.call-done = bf16[1024,4096]{1,0:T(8,128)(2,1)} async-done(((bf16[128,4096]{1,0:T(8,128)(2,1)}), bf16[1024,4096]{1,0:T(8,128)(2,1)}) %all-gather.5.cloned.1.call-update) | async-done | bytes 8388624 | tf_op jit(solution)/shard_map/all_gather | solution.py:195
  195.7 6.4 convolution_bitcast_fusion
  202.1 1.2 subtract_convert_fusion.5
  203.3 5.8 fusion.3
  209.2 163.2 %all-gather.3.cloned.1.call-done = bf16[1024,4096]{1,0:T(8,128)(2,1)} async-done(((bf16[128,4096]{1,0:T(8,128)(2,1)}), bf16[1024,4096]{1,0:T(8,128)(2,1)}) %all-gather.3.cloned.1.call-update) | async-done | bytes 8388624 | tf_op jit(solution)/shard_map/all_gather | solution.py:189
  372.4 8.5 %fusion.5 = f32[1024,4,128]{0,2,1:T(8,128)S(1)} fusion(bf16[4,128,4096]{2,1,0:T(8,128)(2,1)} %bitcast.349, bf16[1024,4096]{1,0:T(8,128)(2,1)} %all-gather.3.cloned.1.call-done), kind=kOutput, calls=%fused_computation.10 | convolution fusion | flops 4294967296 | bytes 14680064 | tf_op jit(solution)/shard_map/dot_general | solution.py:151
  380.9 1.7 subtract_convert_fusion
  382.6 0.9 fusion.24
  383.5 1.0 fusion.27
  384.6 1.4 fusion.81
  386.0 1.2 slice-done.5
  387.5 2.3 convolution_convert_fusion
  389.8 1.8 fusion.15
  391.6 1.4 fusion.42
  393.0 0.8 fusion.85
  394.3 1.6 fusion.8
  395.9 2.3 fusion.11
  398.3 5.3 fusion
  403.5 2.6 fusion.78
  406.2 5.1 fusion.12
  411.3 0.7 fusion.53
  412.1 1.5 fusion.74
  413.8 2.9 convolution_bitcast_fusion.1
  416.8 1.3 fusion.120
  418.9 8.6 %fusion.20 = f32[1024,4096]{1,0:T(8,128)} fusion(bf16[1024,512]{0,1:T(8,128)(2,1)S(1)} %pad_maximum_fusion.1, bf16[1,4096,512]{2,1,0:T(8,128)(2,1)S(1)} %copy-done.6), kind=kOutput, calls=%fused_computation.32 | convolution fusion | flops 4294967296 | bytes 22020096 | tf_op jit(solution)/shard_map/tc,rc->tr/dot_general | solution.py:201
  427.5 8.1 %fusion.86 = f32[1024,4096]{1,0:T(8,128)} fusion(bf16[1024,128]{0,1:T(8,128)(2,1)S(1)} %pad_maximum_fusion.7, bf16[1,4096,128]{2,1,0:T(8,128)(2,1)S(1)} %copy-done), kind=kOutput, calls=%fused_computation.105 | convolution fusion | flops 1073741824 | bytes 18087936 | tf_op jit(solution)/shard_map/tc,rc->tr/dot_general | solution.py:202
  435.6 15.3 %add_convert_fusion = bf16[1024,4096]{1,0:T(8,128)(2,1)} fusion(f32[1024,4096]{1,0:T(8,128)} %fusion.20, f32[1024,4096]{1,0:T(8,128)} %fusion.86, bf16[1024,128]{1,0:T(8,128)(2,1)S(1)} %fusion.78, bf16[1,4096,128]{2,1,0:T(8,128)(2,1)S(1)} %copy-done.11), kind=kOutput, calls=%fused_computation | convolution fusion | flops 1086324736 | bytes 43253760 | tf_op jit(solution)/shard_map/tc,rc->tr/dot_general | solution.py:206
  451.1 0.8 copy-done.17
  452.1 0.9 fusion.23
  453.0 1.0 fusion.25
  454.1 1.6 fusion.7
  455.9 2.3 convolution_convert_fusion.1
  458.3 2.3 fusion.9
  460.6 1.6 fusion.66
  462.1 2.9 fusion.60
  465.8 29.1 %all_to_all.29 = bf16[8,128,512]{2,1,0:T(8,128)(2,1)S(1)} all-to-all(bf16[8,128,512]{2,1,0:T(8,128)(2,1)S(1)} %bitcast.353), channel_id=1, replica_groups=mesh['section'=16,'seq'=8] {'seq'}, dimensions={0} | all-to-all | bytes 2097152 | tf_op jit(solution)/shard_map/all_to_all | solution.py:192
  495.4 0.6 copy-done.3
  496.1 1.2 fusion.32
  497.2 3.3 collective-permute-start
  500.5 147.7 %reduce-scatter.2.cloned.1.call-done = bf16[128,4096]{1,0:T(8,128)(2,1)} async-done(((bf16[1024,4096]{1,0:T(8,128)(2,1)}), bf16[128,4096]{1,0:T(8,128)(2,1)}) %reduce-scatter.2.cloned.1.call-update) | async-done | bytes 1048592 | tf_op jit(solution)/shard_map/reduce_scatter | solution.py:203
  648.2 1.6 fusion.41
  649.9 2.1 fusion.40
  652.0 2.5 collective-permute-start.1
  654.5 13.6 %collective-permute-done.1 = bf16[128,4096]{1,0:T(8,128)(2,1)S(1)} collective-permute-done((bf16[128,4096]{1,0:T(8,128)(2,1)S(1)}, bf16[128,4096]{1,0:T(8,128)(2,1)S(1)}, u32[]{:S(2)}, u32[]{:S(2)}) %collective-permute-start.1) | collective-permute-done | bytes 1048608 | tf_op jit(solution)/shard_map/ppermute | solution.py:15
  668.1 2.3 copy.93
  670.4 1.0 copy.94
  (79 shorter events, 4.8 us)
Async XLA Ops:
  7.2 188.5 %copy-start = (bf16[1,4096,128]{2,1,0:T(8,128)(2,1)S(1)}, bf16[1,4096,128]{2,1,0:T(8,128)(2,1)}, u32[]{:S(2)}) copy-start(bf16[1,4096,128]{2,1,0:T(8,128)(2,1)} %param.28) | copy-start | bytes 3145732
  7.2 8.6 %copy-start.4 = (bf16[1,128,4096]{2,1,0:T(8,128)(2,1)S(1)}, bf16[1,128,4096]{2,1,0:T(8,128)(2,1)}, u32[]{:S(2)}) copy-start(bf16[1,128,4096]{2,1,0:T(8,128)(2,1)} %param.23) | copy-start | bytes 3145732
  7.2 188.5 %all-gather.5.cloned.1.call-start = ((), (), s32[]{:S(2)}) async-start(), calls=%async_computation.4 | async-start | bytes 9437184 | tf_op jit(solution)/shard_map/all_gather | solution.py:195
  10.9 0.6 copy-start.20
  15.0 357.4 %all-gather.3.cloned.1.call-start = ((), (), s32[]{:S(2)}) async-start(), calls=%async_computation.3 | async-start | bytes 9437184 | tf_op jit(solution)/shard_map/all_gather | solution.py:189
  17.6 24.6 %all-to-all-start.1 = ((bf16[128,8,512]{2,0,1:T(8,128)(2,1)}), bf16[128,8,512]{2,0,1:T(8,128)(2,1)S(1)}, u32[]{:S(2)}, u32[]{:S(2)}) async-start(bf16[128,8,512]{2,0,1:T(8,128)(2,1)} %copy.43), calls=%async_computation.1 | async-start | bytes 2097152 | tf_op jit(solution)/shard_map/all_to_all | solution.py:196
  23.8 624.4 %reduce-scatter.2.cloned.1.call-start = ((), (), s32[]{:S(2)}) async-start(), calls=%async_computation.5 | async-start | bytes 9437184 | tf_op jit(solution)/shard_map/reduce_scatter | solution.py:203
  195.7 7.6 %copy-start.1 = (bf16[1024,4096]{1,0:T(8,128)(2,1)S(1)}, bf16[1024,4096]{1,0:T(8,128)(2,1)}, u32[]{:S(2)}) copy-start(bf16[1024,4096]{1,0:T(8,128)(2,1)} %all-gather.5.cloned.1.call-done) | copy-start | bytes 25165828
  195.7 7.6 %copy-start.7 = (bf16[512,4096]{1,0:T(8,128)(2,1)S(1)}, bf16[512,4096]{1,0:T(8,128)(2,1)}, u32[]{:S(2)}) copy-start(bf16[512,4096]{1,0:T(8,128)(2,1)} %copy.76) | copy-start | bytes 12582916
  372.4 8.5 %copy-start.9 = (f32[1024,4,128]{0,2,1:T(8,128)S(1)}, f32[1024,4,128]{0,2,1:T(8,128)}, u32[]{:S(2)}) copy-start(f32[1024,4,128]{0,2,1:T(8,128)} %fusion.3) | copy-start | bytes 6291460
  382.6 2.0 copy-start.16
  383.5 2.5 slice-start.4
  384.6 2.6 slice-start.5
  384.6 2.8 copy-start.10
  395.9 2.3 copy-start.15
  398.3 15.5 %slice-start = ((s8[8388608]{0:T(1024)(128)(4,1)}), s8[4194304]{0:T(1024)(128)(4,1)S(1)}, s32[]{:S(2)}) async-start(s8[8388608]{0:T(1024)(128)(4,1)} %bitcast.340), calls=%async_computation.6 | async-start | bytes 8388608
  403.5 10.3 %slice-start.1 = ((s8[8388608]{0:T(1024)(128)(4,1)}), s8[4194304]{0:T(1024)(128)(4,1)S(1)}, s32[]{:S(2)}) async-start(s8[8388608]{0:T(1024)(128)(4,1)} %bitcast.340), calls=%async_computation.7 | async-start | bytes 8388608
  412.1 1.5 copy-start.13
  412.1 1.5 copy-start.14
  413.8 4.2 copy-start.12
  416.7 2.2 copy-start.6
  427.5 8.1 %copy-start.11 = (bf16[1,4096,128]{2,1,0:T(8,128)(2,1)S(1)}, bf16[1,4096,128]{2,1,0:T(8,128)(2,1)}, u32[]{:S(2)}) copy-start(bf16[1,4096,128]{2,1,0:T(8,128)(2,1)} %param.29) | copy-start | bytes 3145732
  450.9 1.0 copy-start.17
  450.9 1.2 copy-start.18
  452.1 2.0 copy-start.8
  452.1 3.6 slice-start.2
  453.0 2.9 slice-start.3
  494.8 1.2 copy-start.3
  495.1 153.1 %copy-start.2 = (bf16[1,128,4096]{2,1,0:T(8,128)(2,1)S(1)}, bf16[1,128,4096]{2,1,0:T(8,128)(2,1)}, u32[]{:S(2)}) copy-start(bf16[1,128,4096]{2,1,0:T(8,128)(2,1)} %param.22) | copy-start | bytes 3145732
  495.1 153.0 %copy-start.19 = (f32[1,4096]{1,0:T(1,128)S(1)}, f32[1,4096]{1,0:T(1,128)}, u32[]{:S(2)}) copy-start(f32[1,4096]{1,0:T(1,128)} %param.26) | copy-start | bytes 49156
  495.4 154.4 %copy-start.5 = (bf16[1,128,4096]{2,1,0:T(8,128)(2,1)S(1)}, bf16[1,128,4096]{2,1,0:T(8,128)(2,1)}, u32[]{:S(2)}) copy-start(bf16[1,128,4096]{2,1,0:T(8,128)(2,1)} %param.23) | copy-start | bytes 3145732
  495.4 154.4 %copy-start.21 = (f32[128]{0:T(128)S(1)}, f32[128]{0:T(128)}, u32[]{:S(2)}) copy-start(f32[128]{0:T(128)} %copy-done.20) | copy-start | bytes 1540
  495.4 154.4 %copy-start.22 = (f32[128]{0:T(128)S(1)}, f32[128]{0:T(128)}, u32[]{:S(2)}) copy-start(f32[128]{0:T(128)} %get-tuple-element.102) | copy-start | bytes 1540
  497.2 157.2 %collective-permute-start = (bf16[128,4096]{1,0:T(8,128)(2,1)}, bf16[128,4096]{1,0:T(8,128)(2,1)}, u32[]{:S(2)}, u32[]{:S(2)}) collective-permute-start(bf16[128,4096]{1,0:T(8,128)(2,1)} %fusion.32), channel_id=1, source_target_pairs={{0,8},{8,16},{16,24},{24,32},{32,40},{40,48},{48,56},{56,64},{64,7... | collective-permute-start | bytes 3145736 | tf_op jit(solution)/shard_map/ppermute | solution.py:15
  652.0 16.1 %collective-permute-start.1 = (bf16[128,4096]{1,0:T(8,128)(2,1)S(1)}, bf16[128,4096]{1,0:T(8,128)(2,1)S(1)}, u32[]{:S(2)}, u32[]{:S(2)}) collective-permute-start(bf16[128,4096]{1,0:T(8,128)(2,1)S(1)} %fusion.40), channel_id=1, source_target_pairs={{8,0},{16,8},{24,16},{32,24},{40,32},{48,40},{56,48},{64,56},{72,6... | collective-permute-start | bytes 3145736 | tf_op jit(solution)/shard_map/ppermute | solution.py:15
Sparse Core Ops, SparseCore 0:
  15.2 180.4 all-gather.4
  197.9 174.4 all-gather.2
  451.0 197.0 reduce-scatter.1
where the time goes:
time: 681 us; the launch traced here: 678 us
  waiting for transfers between devices  480 us (70%)
  matrix products  84.5 us (12%)
  other arithmetic  34.4 us (5%)
  blocking collectives  29.1 us (4%)
  local copies, waits for them, and re-layouts  23.2 us (3%)
  between operations  14.5 us (2%)
  starting transfers between devices  12.6 us (2%)
    all_gather x1, waiting for transfers between devices, body(): forward_whole = lax.all_gather(forward_normed, 'seq', axis=0, tiled=True)  163 us
    all_gather x1, waiting for transfers between devices, body(): back_whole = lax.all_gather(back_normed, 'seq', axis=0, tiled=True)  149 us
    reduce_scatter x1, waiting for transfers between devices, body(): lax.psum_scatter((term + jnp.einsum('tc,rc->tr', value_grad, weights[2],...  148 us
    all_to_all x1, blocking collectives, body(): lax.all_to_all(mixed_rows, 'seq', split_axis=0, concat_axis=1, tiled=True)  29.1 us
    dot_general x1, matrix products, body(): jnp.einsum('tc,rc->tr', value_grad, weights[2], preferred_element_type=jn...  15.3 us
    dot_general x2, matrix products, heads_inputs(): jnp.dot(rows_whole, query_weight, preferred_element_type=jnp.float32)  14.3 us
  transfers between devices with their start and end apart: 6, of which 5 were waited for; matrix products, arithmetic and copies ran while one was open for 8% of the time, Pallas kernels for 0%

commit v1 on v0

--- a/solution.py
+++ b/solution.py
@@ -7,6 +7,11 @@
 HEAD_SIZE = 128
 epsilon = 1e-05
 rope_base = 500000.0
+
+
+def gather_over(value, mesh_axis, d):
+    sent = jnp.stack([value] * lax.axis_size(mesh_axis))
+    return jnp.concatenate(lax.all_to_all(sent, mesh_axis, 0, 0), axis=d)
 
 
 def passed_along(shard, axis, by):
@@ -186,7 +191,7 @@
     back_hidden = saved_rows[0].astype(jnp.float32)
     back_scale = token_scale(back_hidden)
     back_normed = (back_hidden * back_scale * gain_row).astype(jnp.bfloat16)
-    forward_whole = lax.all_gather(forward_normed, "seq", axis=0, tiled=True)
+    forward_whole = gather_over(forward_normed, "seq", 0)
     query_rows_local, key_rows, value_rows, cosines, sines = heads_inputs(forward_whole, weights)
     mixed_rows = attend(query_rows_local, key_rows, value_rows, first_docs)
     mixed_rows = lax.all_to_all(mixed_rows, "seq", split_axis=0, concat_axis=1, tiled=True)

time: 681 us -> 585 us (0.86)
  waiting for transfers between devices: 480 us -> 365 us
  starting transfers between devices: 12.6 us -> 26.6 us
    all_gather x1 -> x0, waiting for transfers between devices: 163 us -> none  [body(): forward_whole = lax.all_gather(forward_normed, 'seq', axis=0, tiled=True)]
    all_to_all x0 -> x1, waiting for transfers between devices: none -> 122 us  [gather_over(): return jnp.concatenate(lax.all_to_all(sent, mesh_axis, 0, 0), axis=d)]
    all_gather x1, waiting for transfers between devices: 149 us -> 73 us  [body(): back_whole = lax.all_gather(back_normed, 'seq', axis=0, tiled=True)]
    all_to_all x0 -> x1, starting transfers between devices: none -> 13.2 us  [gather_over(): return jnp.concatenate(lax.all_to_all(sent, mesh_axis, 0, 0), axis=d)]
    all_to_all x1, waiting for transfers between devices: 6.01 us -> 14 us  [body(): lax.all_to_all(output_grad[0], 'seq', split_axis=1, concat_axis=0, tiled=...]
  transfers between devices with their start and end apart: 6 -> 6, of which waited for: 5 -> 5; matrix products, arithmetic and copies ran while one was open for 8% -> 12% of each run, Pallas kernels for 0% -> 0%
where the time goes in v1:
time: 585 us; the launch traced here: 581 us
  waiting for transfers between devices  365 us (62%)
  matrix products  88.7 us (15%)
  other arithmetic  33.7 us (6%)
  local copies, waits for them, and re-layouts  28.9 us (5%)
  starting transfers between devices  26.6 us (5%)
  blocking collectives  23.8 us (4%)
  between operations  14.9 us (3%)
    reduce_scatter x1, waiting for transfers between devices, body(): lax.psum_scatter((term + jnp.einsum('tc,rc->tr', value_grad, weights[2],...  144 us
    all_to_all x1, waiting for transfers between devices, gather_over(): return jnp.concatenate(lax.all_to_all(sent, mesh_axis, 0, 0), axis=d)  122 us
    all_gather x1, waiting for transfers between devices, body(): back_whole = lax.all_gather(back_normed, 'seq', axis=0, tiled=True)  73 us
    all_to_all x1, blocking collectives, body(): lax.all_to_all(mixed_rows, 'seq', split_axis=0, concat_axis=1, tiled=True)  23.8 us
    dot_general x1, matrix products, body(): jnp.einsum('tc,rc->tr', value_grad, weights[2], preferred_element_type=jn...  15.4 us
    all_to_all x1, waiting for transfers between devices, body(): lax.all_to_all(output_grad[0], 'seq', split_axis=1, concat_axis=0, tiled=...  14 us
    all_to_all x1, starting transfers between devices, gather_over(): return jnp.concatenate(lax.all_to_all(sent, mesh_axis, 0, 0), axis=d)  13.2 us
    dot_general x2, matrix products, heads_inputs(): jnp.dot(rows_whole, key_matrix, preferred_element_type=jnp.float32)  12.9 us
  transfers between devices with their start and end apart: 6, of which 5 were waited for; matrix products, arithmetic and copies ran while one was open for 12% of the time, Pallas kernels for 0%

profile of v1, /device:TPU:1, one launch (start us, length us, event | category | flops | bytes accessed | tf_op | source)
XLA Modules:
  0.0 581.3 jit_solution(6623867737745150664)
XLA Ops:
  7.2 1.7 fusion.33
  10.0 2.5 fusion.35
  12.9 1.4 copy.94
  14.3 6.2 %all-to-all-start.2 = ((bf16[128,8,512]{2,0,1:T(8,128)(2,1)}), bf16[128,8,512]{2,0,1:T(8,128)(2,1)}, u32[]{:S(2)}, u32[]{:S(2)}) async-start(bf16[128,8,512]{2,0,1:T(8,128)(2,1)} %copy.94), calls=%async_computation.2 | async-start | bytes 2097152 | tf_op jit(solution)/shard_map/all_to_all | solution.py:201
  20.5 0.7 copy.78
  21.7 1.5 fusion.86
  23.3 1.5 copy.79
  24.8 14.0 %all-to-all-done.2 = bf16[128,8,512]{2,0,1:T(8,128)(2,1)} async-done(((bf16[128,8,512]{2,0,1:T(8,128)(2,1)}), bf16[128,8,512]{2,0,1:T(8,128)(2,1)}, u32[]{:S(2)}, u32[]{:S(2)}) %all-to-all-start.2) | async-done | bytes 1048608 | tf_op jit(solution)/shard_map/all_to_all | solution.py:201
  38.7 4.4 stack.5
  43.1 13.2 %all-to-all-start = ((bf16[8,128,4096]{2,1,0:T(8,128)(2,1)}), bf16[8,128,4096]{2,1,0:T(8,128)(2,1)}, u32[]{:S(2)}, u32[]{:S(2)}) async-start(bf16[8,128,4096]{2,1,0:T(8,128)(2,1)} %stack.5), calls=%async_computation | async-start | bytes 16777216 | tf_op jit(solution)/shard_map/all_to_all | solution.py:14
  56.5 6.5 %copy.128 = bf16[512,4096]{1,0:T(8,128)(2,1)} copy(bf16[512,4096]{0,1:T(8,128)(2,1)} %bitcast.349) | data formatting | bytes 8388608 | tf_op jit(solution)/shard_map/dot_general | solution.py:156
  63.0 0.8 constant_dynamic-slice_fusion.2
  63.8 0.9 constant_dynamic-slice_fusion
  64.9 1.0 fusion.113
  65.8 0.8 slice_multiply_fusion.1
  66.6 1.0 fusion.48
  67.7 2.1 fusion.147
  69.8 2.0 reshape.548
  71.8 0.9 reshape.550
  72.7 121.9 %all-to-all-done = bf16[8,128,4096]{2,1,0:T(8,128)(2,1)} async-done(((bf16[8,128,4096]{2,1,0:T(8,128)(2,1)}), bf16[8,128,4096]{2,1,0:T(8,128)(2,1)}, u32[]{:S(2)}, u32[]{:S(2)}) %all-to-all-start) | async-done | bytes 8388640 | tf_op jit(solution)/shard_map/all_to_all | solution.py:14
  194.6 6.4 %convolution_bitcast_fusion.1 = f32[1024,1,128]{0,2,1:T(8,128)S(1)} fusion(bf16[1024,4096]{1,0:T(8,128)(2,1)} %bitcast.3, bf16[1,4096,128]{2,1,0:T(8,128)(2,1)S(1)} %copy-done), kind=kOutput, calls=%fused_computation.83 | convolution fusion | flops 1073741824 | bytes 9961472 | tf_op jit(solution)/shard_map/dot_general | solution.py:157
  201.0 8.3 %fusion.149 = f32[1024,4,128]{0,2,1:T(8,128)} fusion(bf16[1024,4096,1]{1,0,2:T(8,128)(2,1)} %bitcast.11, bf16[4,128,4096]{2,1,0:T(8,128)(2,1)S(1)} %bitcast.350), kind=kOutput, calls=%fused_computation.199 | convolution fusion | flops 4294967296 | bytes 14680064 | tf_op jit(solution)/shard_map/dot_general | solution.py:156
  209.4 73.0 %all-gather.2.cloned.1.call-done = bf16[1024,4096]{1,0:T(8,128)(2,1)} async-done(((bf16[128,4096]{1,0:T(8,128)(2,1)}), bf16[1024,4096]{1,0:T(8,128)(2,1)}) %all-gather.2.cloned.1.call-update) | async-done | bytes 8388624 | tf_op jit(solution)/shard_map/all_gather | solution.py:200
  282.3 6.4 %convolution_bitcast_fusion = f32[1024,1,128]{0,2,1:T(8,128)S(1)} fusion(bf16[1024,4096]{1,0:T(8,128)(2,1)} %all-gather.2.cloned.1.call-done, bf16[1,4096,128]{2,1,0:T(8,128)(2,1)S(1)} %copy-done), kind=kOutput, calls=%fused_computation.82 | convolution fusion | flops 1073741824 | bytes 9961472 | tf_op jit(solution)/shard_map/dot_general | solution.py:157
  288.8 1.4 subtract_convert_fusion.5
  290.2 4.5 fusion.3
  294.7 1.7 subtract_convert_fusion
  296.4 0.9 fusion.22
  297.3 1.1 fusion.25
  298.4 2.1 fusion.81
  300.5 2.3 convolution_convert_fusion
  302.8 1.7 fusion.13
  304.6 1.9 fusion.42
  306.5 0.8 fusion.85
  307.7 1.7 fusion.6
  309.4 2.1 fusion.9
  311.6 3.5 fusion
  315.1 2.7 fusion.78
  317.8 2.9 fusion.10
  320.7 0.7 fusion.53
  321.5 1.5 fusion.74
  323.3 2.1 fusion.121
  325.8 8.2 %fusion.18 = f32[1024,4096]{1,0:T(8,128)} fusion(bf16[1024,512]{0,1:T(8,128)(2,1)S(1)} %pad_maximum_fusion.1, bf16[1,4096,512]{2,1,0:T(8,128)(2,1)S(1)} %copy-done.6), kind=kOutput, calls=%fused_computation.30 | convolution fusion | flops 4294967296 | bytes 22020096 | tf_op jit(solution)/shard_map/tc,rc->tr/dot_general | solution.py:206
  334.0 8.1 %fusion.87 = f32[1024,4096]{1,0:T(8,128)} fusion(bf16[1024,128]{0,1:T(8,128)(2,1)S(1)} %pad_maximum_fusion.7, bf16[1,4096,128]{2,1,0:T(8,128)(2,1)S(1)} %copy-done), kind=kOutput, calls=%fused_computation.104 | convolution fusion | flops 1073741824 | bytes 18087936 | tf_op jit(solution)/shard_map/tc,rc->tr/dot_general | solution.py:207
  342.1 15.4 %add_convert_fusion = bf16[1024,4096]{1,0:T(8,128)(2,1)} fusion(f32[1024,4096]{1,0:T(8,128)} %fusion.18, f32[1024,4096]{1,0:T(8,128)} %fusion.87, bf16[1024,128]{1,0:T(8,128)(2,1)S(1)} %fusion.78, bf16[1,4096,128]{2,1,0:T(8,128)(2,1)S(1)} %copy-done.12), kind=kOutput, calls=%fused_computation | convolution fusion | flops 1086324736 | bytes 43253760 | tf_op jit(solution)/shard_map/tc,rc->tr/dot_general | solution.py:211
  357.7 5.8 convolution_convert_fusion.1
  363.6 0.9 fusion.21
  364.5 1.1 fusion.23
  365.6 1.7 fusion.5
  367.2 2.3 fusion.7
  369.6 1.5 fusion.66
  371.1 2.9 fusion.60
  374.2 1.3 copy.89
  375.5 23.8 %all_to_all.34 = bf16[8,128,512]{2,1,0:T(8,128)(2,1)} all-to-all(bf16[8,128,512]{2,1,0:T(8,128)(2,1)} %bitcast.353), channel_id=1, replica_groups=mesh['section'=16,'seq'=8] {'seq'}, dimensions={0} | all-to-all | bytes 2097152 | tf_op jit(solution)/shard_map/all_to_all | solution.py:197
  399.4 2.3 copy.90
  401.6 2.5 fusion.30
  404.1 4.5 collective-permute-start
  408.6 144.5 %reduce-scatter.2.cloned.1.call-done = bf16[128,4096]{1,0:T(8,128)(2,1)} async-done(((bf16[1024,4096]{1,0:T(8,128)(2,1)}), bf16[128,4096]{1,0:T(8,128)(2,1)}) %reduce-scatter.2.cloned.1.call-update) | async-done | bytes 1048592 | tf_op jit(solution)/shard_map/reduce_scatter | solution.py:208
  553.1 1.6 fusion.41
  554.7 2.4 fusion.40
  557.2 2.5 collective-permute-start.1
  559.7 2.3 copy.105
  562.0 11.3 %collective-permute-done.1 = bf16[128,4096]{1,0:T(8,128)(2,1)S(1)} collective-permute-done((bf16[128,4096]{1,0:T(8,128)(2,1)S(1)}, bf16[128,4096]{1,0:T(8,128)(2,1)S(1)}, u32[]{:S(2)}, u32[]{:S(2)}) %collective-permute-start.1) | collective-permute-done | bytes 1048608 | tf_op jit(solution)/shard_map/ppermute | solution.py:20
  573.3 1.0 copy.143
  (81 shorter events, 4.1 us)
Async XLA Ops:
  7.2 187.4 %copy-start = (bf16[1,4096,128]{2,1,0:T(8,128)(2,1)S(1)}, bf16[1,4096,128]{2,1,0:T(8,128)(2,1)}, u32[]{:S(2)}) copy-start(bf16[1,4096,128]{2,1,0:T(8,128)(2,1)} %param.28) | copy-start | bytes 3145732
  7.2 5.3 copy-start.5
  7.2 275.1 %all-gather.2.cloned.1.call-start = ((), (), s32[]{:S(2)}) async-start(), calls=%async_computation.4 | async-start | bytes 9437184 | tf_op jit(solution)/shard_map/all_gather | solution.py:200
  9.4 0.5 copy-start.24
  12.5 8.0 %copy-start.10 = (bf16[1,128,4096]{2,1,0:T(8,128)(2,1)S(1)}, bf16[1,128,4096]{2,1,0:T(8,128)(2,1)}, u32[]{:S(2)}) copy-start(bf16[1,128,4096]{2,1,0:T(8,128)(2,1)} %param.21) | copy-start | bytes 3145732
  12.9 8.8 %copy-start.20 = (f32[1,4096]{1,0:T(1,128)S(1)}, f32[1,4096]{1,0:T(1,128)}, u32[]{:S(2)}) copy-start(f32[1,4096]{1,0:T(1,128)} %param.26) | copy-start | bytes 49156
  14.3 24.4 %all-to-all-start.2 = ((bf16[128,8,512]{2,0,1:T(8,128)(2,1)}), bf16[128,8,512]{2,0,1:T(8,128)(2,1)}, u32[]{:S(2)}, u32[]{:S(2)}) async-start(bf16[128,8,512]{2,0,1:T(8,128)(2,1)} %copy.94), calls=%async_computation.2 | async-start | bytes 2097152 | tf_op jit(solution)/shard_map/all_to_all | solution.py:201
  21.2 21.9 %copy-start.3 = (bf16[1,128,4096]{1,2,0:T(8,128)(2,1)}, bf16[1,128,4096]{1,2,0:T(8,128)(2,1)S(1)}, u32[]{:S(2)}) copy-start(bf16[1,128,4096]{1,2,0:T(8,128)(2,1)S(1)} %copy.78) | copy-start | bytes 3145732
  43.1 151.5 %all-to-all-start = ((bf16[8,128,4096]{2,1,0:T(8,128)(2,1)}), bf16[8,128,4096]{2,1,0:T(8,128)(2,1)}, u32[]{:S(2)}, u32[]{:S(2)}) async-start(bf16[8,128,4096]{2,1,0:T(8,128)(2,1)} %stack.5), calls=%async_computation | async-start | bytes 16777216 | tf_op jit(solution)/shard_map/all_to_all | solution.py:14
  56.3 496.8 %reduce-scatter.2.cloned.1.call-start = ((), (), s32[]{:S(2)}) async-start(), calls=%async_computation.5 | async-start | bytes 9437184 | tf_op jit(solution)/shard_map/reduce_scatter | solution.py:208
  194.6 6.4 %copy-start.7 = (bf16[512,4096]{1,0:T(8,128)(2,1)S(1)}, bf16[512,4096]{1,0:T(8,128)(2,1)}, u32[]{:S(2)}) copy-start(bf16[512,4096]{1,0:T(8,128)(2,1)} %copy.128) | copy-start | bytes 12582916
  282.3 7.8 %copy-start.1 = (bf16[1024,4096]{1,0:T(8,128)(2,1)S(1)}, bf16[1024,4096]{1,0:T(8,128)(2,1)}, u32[]{:S(2)}) copy-start(bf16[1024,4096]{1,0:T(8,128)(2,1)} %all-gather.2.cloned.1.call-done) | copy-start | bytes 25165828
  282.3 7.8 %copy-start.8 = (bf16[512,4096]{1,0:T(8,128)(2,1)S(1)}, bf16[512,4096]{1,0:T(8,128)(2,1)}, u32[]{:S(2)}) copy-start(bf16[512,4096]{1,0:T(8,128)(2,1)} %copy.128) | copy-start | bytes 12582916
  290.2 4.5 copy-start.9
  296.4 2.0 copy-start.17
  298.4 2.1 copy-start.11
  302.8 1.8 copy-start.27
  309.4 2.1 copy-start.16
  309.4 2.1 copy-start.28
  311.6 3.5 copy-start.29
  321.5 1.5 copy-start.14
  321.5 1.5 copy-start.15
  321.5 3.9 copy-start.13
  323.2 2.6 copy-start.6
  334.0 8.1 %copy-start.12 = (bf16[1,4096,128]{2,1,0:T(8,128)(2,1)S(1)}, bf16[1,4096,128]{2,1,0:T(8,128)(2,1)}, u32[]{:S(2)}) copy-start(bf16[1,4096,128]{2,1,0:T(8,128)(2,1)} %param.29) | copy-start | bytes 3145732
  357.7 5.9 %copy-start.18 = (bf16[1024,4,64]{0,2,1:T(8,128)(2,1)S(1)}, bf16[1024,4,64]{0,2,1:T(8,128)(2,1)}, u32[]{:S(2)}) copy-start(bf16[1024,4,64]{0,2,1:T(8,128)(2,1)} %get-tuple-element.90) | copy-start | bytes 1572868
  357.7 5.8 %copy-start.19 = (bf16[1024,4,64]{0,2,1:T(8,128)(2,1)S(1)}, bf16[1024,4,64]{0,2,1:T(8,128)(2,1)}, u32[]{:S(2)}) copy-start(bf16[1024,4,64]{0,2,1:T(8,128)(2,1)} %get-tuple-element.91) | copy-start | bytes 1572868
  357.7 5.8 %copy-start.22 = (bf16[1024,1,64]{0,2,1:T(8,128)(2,1)S(1)}, bf16[1024,1,64]{0,2,1:T(8,128)(2,1)}, u32[]{:S(2)}) copy-start(bf16[1024,1,64]{0,2,1:T(8,128)(2,1)} %get-tuple-element.104) | copy-start | bytes 393220
  357.7 5.8 %copy-start.23 = (bf16[1024,1,64]{0,2,1:T(8,128)(2,1)S(1)}, bf16[1024,1,64]{0,2,1:T(8,128)(2,1)}, u32[]{:S(2)}) copy-start(bf16[1024,1,64]{0,2,1:T(8,128)(2,1)} %get-tuple-element.105) | copy-start | bytes 393220
  374.0 27.6 %copy-start.4 = (bf16[1,128,4096]{1,2,0:T(8,128)(2,1)S(1)}, bf16[1,128,4096]{1,2,0:T(8,128)(2,1)}, u32[]{:S(2)}) copy-start(bf16[1,128,4096]{1,2,0:T(8,128)(2,1)} %copy-done.3) | copy-start | bytes 3145732
  375.5 177.5 %copy-start.2 = (bf16[1,128,4096]{2,1,0:T(8,128)(2,1)S(1)}, bf16[1,128,4096]{2,1,0:T(8,128)(2,1)}, u32[]{:S(2)}) copy-start(bf16[1,128,4096]{2,1,0:T(8,128)(2,1)} %param.22) | copy-start | bytes 3145732
  375.5 177.5 %copy-start.21 = (f32[1,4096]{1,0:T(1,128)S(1)}, f32[1,4096]{1,0:T(1,128)}, u32[]{:S(2)}) copy-start(f32[1,4096]{1,0:T(1,128)} %param.26) | copy-start | bytes 49156
  399.4 155.3 %copy-start.25 = (f32[128]{0:T(128)S(1)}, f32[128]{0:T(128)}, u32[]{:S(2)}) copy-start(f32[128]{0:T(128)} %copy-done.24) | copy-start | bytes 1540
  399.4 155.4 %copy-start.26 = (f32[128]{0:T(128)S(1)}, f32[128]{0:T(128)}, u32[]{:S(2)}) copy-start(f32[128]{0:T(128)} %get-tuple-element.102) | copy-start | bytes 1540
  404.1 155.6 %collective-permute-start = (bf16[128,4096]{0,1:T(8,128)(2,1)}, bf16[128,4096]{0,1:T(8,128)(2,1)}, u32[]{:S(2)}, u32[]{:S(2)}) collective-permute-start(bf16[128,4096]{0,1:T(8,128)(2,1)} %fusion.30), channel_id=1, source_target_pairs={{0,8},{8,16},{16,24},{24,32},{32,40},{40,48},{48,56},{56,64},{64,7... | collective-permute-start | bytes 3145736 | tf_op jit(solution)/shard_map/ppermute | solution.py:20
  557.2 16.1 %collective-permute-start.1 = (bf16[128,4096]{1,0:T(8,128)(2,1)S(1)}, bf16[128,4096]{1,0:T(8,128)(2,1)S(1)}, u32[]{:S(2)}, u32[]{:S(2)}) collective-permute-start(bf16[128,4096]{1,0:T(8,128)(2,1)S(1)} %fusion.40), channel_id=1, source_target_pairs={{8,0},{16,8},{24,16},{32,24},{40,32},{48,40},{56,48},{64,56},{72,6... | collective-permute-start | bytes 3145736 | tf_op jit(solution)/shard_map/ppermute | solution.py:20
Sparse Core Ops, SparseCore 0:
  12.6 269.6 all-gather.1
  357.6 195.4 reduce-scatter.1
